TPU v7x, 256 devices: a whole 4x4x8 slice. The times are simulated.
256 devices in a mesh: dp: 32 (over y_hi, z, core), fsdp: 8 (over x, y_lo).
Axes of the slice: x: 4, y: 4 (y_hi: 2, y_lo: 2; y = y_hi * 2 + y_lo), z: 8, core: 2. Of those that a mesh axis runs over, the one named last changes fastest.
Arguments:
- tokens: bfloat16 [4096, 4096], P(('fsdp', 'dp')), may hold values from -6 to 6
- upstream: bfloat16 [4096, 4096], P(('fsdp', 'dp')), may hold values from -0.375 to 0.375
- old_master: float32 [4096, 3, 5632], P(('fsdp', 'dp')), may hold values from -0.09375 to 0.09375
- old_first: float32 [4096, 3, 5632], P(('fsdp', 'dp')), may hold values from -3 to 3
- old_second: float32 [4096, 3, 5632], P(('fsdp', 'dp')), may hold values from 0.01 to 4
- grown_master: float32 [4096, 3, 2560], P(('fsdp', 'dp')), may hold values from -0.09375 to 0.09375
- grown_first: float32 [4096, 3, 2560], P(('fsdp', 'dp')), may hold values from -3 to 3
- grown_second: float32 [4096, 3, 2560], P(('fsdp', 'dp')), may hold values from 0.01 to 4
- grow_mask: float32 [2560], replicated, may hold values from 0.1 to 1
Outputs:
- layer_output: bfloat16 [4096, 4096], P(('fsdp', 'dp'))
- new_master: float32 [4096, 3, 8192], P('fsdp', None, 'dp')
- new_first: float32 [4096, 3, 8192], P('fsdp', None, 'dp')
- new_second: float32 [4096, 3, 8192], P('fsdp', None, 'dp')
All inputs are finite; a program needn't handle non-finite values.
Results may differ from a plain program's by a relative error of at most 0.019.
Values may be sent and summed in bfloat16 or wider, within the bound.
A program may use at most 128 MiB of HBM per device.

v0:
```python
import jax
import jax.numpy as jnp
from jax import lax
from jax.sharding import PartitionSpec as P

STEP = 1000
beta_first = 0.9
beta_second = 0.999
adam_epsilon = 1e-08
learn_rate = 0.001
weight_decay = 0.1


def sent_together(arrays, axis, dim, along):
    both = jnp.concatenate(arrays, axis=along)
    filled, at, gathered = (lax.all_gather(both, axis, axis=dim, tiled=True), 0, [])
    for a in arrays:
        gathered.append(lax.slice_in_dim(filled, at, at + a.shape[along], axis=along))
        at += a.shape[along]
    return tuple(gathered)


def split_up(array, dim, size):
    lengths = array.shape
    parts = array.reshape(*lengths[:dim], size, lengths[dim] // size, *lengths[dim + 1 :])
    return jnp.moveaxis(parts, dim, 0)


def sent_and_summed(array, axis, dim):
    parts = split_up(array, dim, lax.axis_size(axis))
    arrived = lax.all_to_all(parts, axis, split_axis=0, concat_axis=0, tiled=True)
    return arrived.astype(jnp.float32).sum(axis=0)


def in_one_piece(arrays, axis, split_dim, concat_dim, along):
    both = jnp.concatenate(arrays, axis=along)
    filled, at, gathered = (
        lax.all_to_all(both, axis, split_axis=split_dim, concat_axis=concat_dim, tiled=True),
        0,
        [],
    )
    for a in arrays:
        gathered.append(lax.slice_in_dim(filled, at, at + a.shape[along], axis=along))
        at += a.shape[along]
    return tuple(gathered)


def contract_rows(left_part, right_part):
    return lax.dot_general(
        left_part, right_part, (((0,), (0,)), ((), ())), preferred_element_type=jnp.float32
    )


def contract_last(left_part, right_part):
    return lax.dot_general(
        left_part, right_part, (((1,), (1,)), ((), ())), preferred_element_type=jnp.float32
    )


def adam_update(master, first_moment, second_moment, gradients):
    new_first = beta_first * first_moment + (1.0 - beta_first) * gradients
    new_second = beta_second * second_moment + (1.0 - beta_second) * gradients * gradients
    first_hat = new_first / (1.0 - beta_first**STEP)
    second_hat = new_second / (1.0 - beta_second**STEP)
    new_master = master - learn_rate * (
        first_hat / (jnp.sqrt(second_hat) + adam_epsilon) + weight_decay * master
    )
    return (new_master, new_first, new_second)


def local(
    tokens,
    upstream,
    old_master,
    old_first,
    old_second,
    grown_master,
    grown_first,
    grown_second,
    grow_mask,
):
    new_width = old_master.shape[2] + grown_master.shape[2]
    block_width = new_width // lax.axis_size("dp")
    master_all = jnp.concatenate([old_master, grown_master], axis=2)
    first_all = jnp.concatenate([old_first, grown_first], axis=2)
    second_all = jnp.concatenate([old_second, grown_second], axis=2)
    master = lax.all_to_all(
        master_all.astype(jnp.bfloat16), "dp", split_axis=2, concat_axis=0, tiled=True
    ).astype(master_all.dtype)
    weights = lax.all_gather(master.astype(jnp.bfloat16), "fsdp", axis=0, tiled=True)
    rows_in, rows_back = sent_together((tokens, upstream), "dp", 0, 1)
    all_scales = jnp.concatenate([jnp.ones((old_master.shape[2],), jnp.float32), grow_mask])
    scales = lax.dynamic_slice_in_dim(all_scales, lax.axis_index("dp") * block_width, block_width)
    model_width = weights.shape[0]
    paired = weights[:, :2, :].reshape(model_width, 2 * block_width)
    down_weights = weights[:, 2, :]
    projected = jnp.dot(rows_in, paired, preferred_element_type=jnp.float32)
    gate_value = projected[:, :block_width]
    up_value = projected[:, block_width:]
    sigmoid_gate = jax.nn.sigmoid(gate_value)
    activated = gate_value * sigmoid_gate
    hidden = (activated * up_value * scales).astype(jnp.bfloat16)
    summed = lax.psum_scatter(
        contract_last(hidden, down_weights).astype(jnp.bfloat16),
        "dp",
        scatter_dimension=0,
        tiled=True,
    )
    back_hidden = jnp.dot(rows_back, down_weights, preferred_element_type=jnp.float32) * scales
    own_rows = master.shape[0]
    down_grad = sent_and_summed(contract_rows(rows_back, hidden).astype(jnp.bfloat16), "fsdp", 0)
    gate_back = (
        back_hidden * up_value * sigmoid_gate * (1.0 + gate_value * (1.0 - sigmoid_gate))
    ).astype(jnp.bfloat16)
    up_back = (back_hidden * activated).astype(jnp.bfloat16)
    inner_back = jnp.concatenate([gate_back, up_back], axis=1)
    inner_grad = sent_and_summed(contract_rows(rows_in, inner_back).astype(jnp.bfloat16), "fsdp", 0)
    gradients = jnp.concatenate(
        [inner_grad.reshape(own_rows, 2, block_width), down_grad[:, None, :]], axis=1
    )
    first_moment, second_moment = tuple(
        (
            part.astype(jnp.float32)
            for part in in_one_piece(
                (first_all.astype(jnp.bfloat16), second_all.astype(jnp.bfloat16)), "dp", 2, 0, 1
            )
        )
    )
    new_master, new_first, new_second = adam_update(master, first_moment, second_moment, gradients)
    return (summed, new_master, new_first, new_second)


def solution(mesh):
    in_specs = (
        P(("fsdp", "dp"), None),
        P(("fsdp", "dp"), None),
        P(("fsdp", "dp"), None, None),
        P(("fsdp", "dp"), None, None),
        P(("fsdp", "dp"), None, None),
        P(("fsdp", "dp"), None, None),
        P(("fsdp", "dp"), None, None),
        P(("fsdp", "dp"), None, None),
        P(),
    )
    out_specs = (
        P(("fsdp", "dp"), None),
        P("fsdp", None, "dp"),
        P("fsdp", None, "dp"),
        P("fsdp", None, "dp"),
    )
    return jax.shard_map(local, mesh=mesh, in_specs=in_specs, out_specs=out_specs, check_vma=False)
```

profile of v0, /device:TPU:4, one launch (start us, length us, event | category | flops | bytes accessed | tf_op | source)
XLA Modules:
  0.0 517.3 jit_solution(11075435288912256371)
XLA Ops:
  7.2 0.0 all-gather.5.cloned.1.call-start
  7.2 1.1 convert.19
  8.3 1.3 convert.18
  9.6 0.1 pad_maximum_fusion.1
  9.6 8.3 %copy.39 = bf16[16,3,8192]{0,1,2:T(4,128)(2,1)} copy(bf16[16,3,8192]{2,0,1:T(8,128)(2,1)S(1)} %pad_maximum_fusion.1) | data formatting | bytes 1572864 | tf_op jit(solution)/shard_map/concatenate | solution.py:84
  17.9 12.8 %reshape.25 = bf16[32,2,6144]{2,1,0:T(2,128)(2,1)S(1)} reshape(bf16[8192,3,16]{2,1,0:T(4,128)(2,1)} %bitcast.33) | data formatting | bytes 1572864
  30.7 36.1 %all_to_all.46 = bf16[32,2,6144]{2,1,0:T(2,128)(2,1)S(1)} all-to-all(bf16[32,2,6144]{2,1,0:T(2,128)(2,1)S(1)} %reshape.25), channel_id=1, replica_groups=mesh['dp'=32,'fsdp'=8] {'dp'}, dimensions={0} | all-to-all | bytes 1572864 | tf_op jit(solution)/shard_map/all_to_all | solution.py:87
  66.8 10.7 %reshape.26 = bf16[8192,3,16]{2,1,0:T(4,128)(2,1)} reshape(bf16[32,2,6144]{2,1,0:T(2,128)(2,1)S(1)} %all_to_all.46) | data formatting | bytes 1572864
  77.5 0.0 copy-start.7
  77.5 0.0 copy-start.8
  77.5 0.0 copy-start.5
  77.5 10.9 %copy.49 = bf16[16,3,32,256]{3,0,2,1:T(8,128)(2,1)} copy(bf16[16,3,32,256]{0,1,3,2:T(4,128)(2,1)} %bitcast.34) | data formatting | bytes 1572864 | tf_op jit(solution)/shard_map/all_to_all | solution.py:87
  88.5 0.0 copy-start.3
  88.5 0.0 copy-start.6
  88.5 0.0 all-gather.5.cloned.1.call-update
  88.5 0.0 copy-start.4
  88.5 0.0 all-gather.3.cloned.1.call-start
  88.5 0.0 copy-done.7
  88.5 0.0 copy-done.8
  88.6 0.7 pad_maximum_fusion.2
  89.3 0.0 all-gather.3.cloned.1.call-update
  89.3 0.0 copy-done.5
  89.4 0.4 copy-done.3
  89.8 0.1 convert.22
  89.8 0.1 copy-done.6
  89.9 0.3 copy-done.4
  90.3 0.1 convert.20
  90.3 0.1 maximum_maximum_fusion
  90.5 13.0 %copy.43 = bf16[16,6,8192]{0,1,2:T(8,128)(2,1)} copy(bf16[16,6,8192]{2,0,1:T(8,128)(2,1)S(1)} %maximum_maximum_fusion) | data formatting | bytes 3145728 | tf_op jit(solution)/shard_map/concatenate | solution.py:36
  103.5 18.7 %reshape.27 = bf16[32,2,12288]{2,1,0:T(2,128)(2,1)} reshape(bf16[8192,6,16]{2,1,0:T(8,128)(2,1)} %bitcast.31) | data formatting | bytes 3145728
  122.2 0.0 copy-start.9
  122.2 4.1 all-to-all-start.1
  126.4 0.0 copy-done.9
  126.4 0.1 pad_dynamic-slice_fusion
  126.4 105.6 %all-gather.5.cloned.1.call-done = bf16[4096,3,256]{2,0,1:T(8,128)(2,1)} async-done(((bf16[512,3,256]{2,0,1:T(8,128)(2,1)}), bf16[4096,3,256]{2,0,1:T(8,128)(2,1)}) %all-gather.5.cloned.1.call-update) | async-done | bytes 6291472 | tf_op jit(solution)/shard_map/all_gather | solution.py:90
  232.1 4.4 slice.33
  236.5 6.5 %copy.42 = bf16[4096,2,256]{0,2,1:T(8,128)(2,1)} copy(bf16[4096,2,256]{2,0,1:T(8,128)(2,1)} %slice.33) | data formatting | bytes 8388608 | tf_op jit(solution)/shard_map/slice | solution.py:95
  243.0 95.1 %all-gather.3.cloned.1.call-done = bf16[512,8192]{1,0:T(8,128)(2,1)} async-done(((bf16[16,8192]{1,0:T(8,128)(2,1)}), bf16[512,8192]{1,0:T(8,128)(2,1)}) %all-gather.3.cloned.1.call-update) | async-done | bytes 8388624 | tf_op jit(solution)/shard_map/all_gather | solution.py:16
  338.1 6.0 %fusion.4 = f32[512,512]{0,1:T(8,128)S(1)} fusion(bf16[4096,512]{0,1:T(8,128)(2,1)} %bitcast.38, bf16[512,8192]{1,0:T(8,128)(2,1)} %all-gather.3.cloned.1.call-done), kind=kOutput, calls=%fused_computation.9 | convolution fusion | flops 2147483648 | bytes 9437184 | tf_op jit(solution)/shard_map/dot_general | solution.py:97
  344.0 0.0 copy-done.10
  344.0 3.1 multiply_convert_fusion.1
  347.2 2.7 convolution_convert_fusion.2
  349.8 0.0 all-to-all-done.1
  349.8 1.1 copy-done.1
  351.0 4.8 all-to-all-start.3
  355.8 0.0 reduce-scatter.2.cloned.1.call-start
  355.8 4.8 convolution_convert_fusion
  360.6 0.0 reduce-scatter.2.cloned.1.call-update
  360.7 6.6 %convolution_convert_fusion.1 = bf16[4096,512]{1,0:T(8,128)(2,1)} fusion(bf16[512,8192]{1,0:T(8,128)(2,1)} %all-gather.3.cloned.1.call-done, bf16[512,256]{0,1:T(8,128)(2,1)S(1)} %get-tuple-element.12, bf16[512,256]{0,1:T(8,128)(2,1)S(1)} %get-tuple-element.11), kind=kOutput, calls=%fused_computation.2 | convolution fusion | flops 2150629376 | bytes 8912896 | tf_op jit(solution)/shard_map/dot_general | solution.py:49
  367.2 16.5 %all-to-all-done.3 = bf16[8,512,256]{2,1,0:T(8,128)(2,1)S(1)} async-done(((bf16[8,512,256]{2,1,0:T(8,128)(2,1)}), bf16[8,512,256]{2,1,0:T(8,128)(2,1)S(1)}, u32[]{:S(2)}, u32[]{:S(2)}) %all-to-all-start.3) | async-done | bytes 2097184 | tf_op jit(solution)/shard_map/all_to_all | solution.py:31
  383.7 8.4 %all-to-all-start.2 = ((bf16[8,512,512]{2,1,0:T(8,128)(2,1)}), bf16[8,512,512]{2,1,0:T(8,128)(2,1)}, u32[]{:S(2)}, u32[]{:S(2)}) async-start(bf16[8,512,512]{2,1,0:T(8,128)(2,1)} %bitcast.37), calls=%async_computation.3 | async-start | bytes 8388608 | tf_op jit(solution)/shard_map/all_to_all | solution.py:31
  392.1 18.0 %reshape.28 = bf16[8192,6,16]{2,1,0:T(8,128)(2,1)} reshape(bf16[32,2,12288]{2,1,0:T(2,128)(2,1)} %copy-done.1) | data formatting | bytes 3145728
  410.1 15.1 %copy.45 = bf16[32,16,6,256]{3,1,0,2:T(8,128)(2,1)} copy(bf16[32,16,6,256]{1,2,3,0:T(8,128)(2,1)} %bitcast.32) | data formatting | bytes 3145728 | tf_op jit(solution)/shard_map/all_to_all | solution.py:38
  425.2 1.1 convert_reduce_fusion.1
  426.3 21.5 %all-to-all-done.2 = bf16[8,512,512]{2,1,0:T(8,128)(2,1)} async-done(((bf16[8,512,512]{2,1,0:T(8,128)(2,1)}), bf16[8,512,512]{2,1,0:T(8,128)(2,1)}, u32[]{:S(2)}, u32[]{:S(2)}) %all-to-all-start.2) | async-done | bytes 4194336 | tf_op jit(solution)/shard_map/all_to_all | solution.py:31
  447.8 2.9 convert_reduce_fusion
  450.7 0.0 copy-start
  450.7 0.0 copy-start.2
  450.7 1.3 copy.46
  452.0 1.6 copy.47
  453.6 0.0 copy-done
  453.6 0.0 copy-done.2
  453.6 4.0 convert_subtract_fusion
  457.6 53.1 %reduce-scatter.2.cloned.1.call-done = bf16[16,4096]{1,0:T(8,128)(2,1)} async-done(((bf16[512,4096]{1,0:T(8,128)(2,1)}), bf16[16,4096]{1,0:T(8,128)(2,1)}) %reduce-scatter.2.cloned.1.call-update) | async-done | bytes 131088 | tf_op jit(solution)/shard_map/reduce_scatter | solution.py:103
  (4 shorter events, 0.1 us)
Async XLA Ops:
  7.2 224.9 %all-gather.5.cloned.1.call-start = ((), (), s32[]{:S(2)}) async-start(), calls=%async_computation.6 | async-start | bytes 7077888 | tf_op jit(solution)/shard_map/all_gather | solution.py:90
  77.5 11.0 %copy-start.7 = (bf16[16,4096]{1,0:T(8,128)(2,1)S(1)}, bf16[16,4096]{1,0:T(8,128)(2,1)}, u32[]{:S(2)}) copy-start(bf16[16,4096]{1,0:T(8,128)(2,1)} %param.10) | copy-start | bytes 393220
  77.5 11.0 %copy-start.8 = (bf16[16,4096]{1,0:T(8,128)(2,1)S(1)}, bf16[16,4096]{1,0:T(8,128)(2,1)}, u32[]{:S(2)}) copy-start(bf16[16,4096]{1,0:T(8,128)(2,1)} %param.9) | copy-start | bytes 393220
  77.5 11.8 %copy-start.5 = (f32[16,3,2560]{2,0,1:T(8,128)S(1)}, f32[16,3,2560]{2,0,1:T(8,128)}, u32[]{:S(2)}) copy-start(f32[16,3,2560]{2,0,1:T(8,128)} %param.16) | copy-start | bytes 1474564
  88.5 1.3 copy-start.3
  88.5 1.4 copy-start.6
  88.5 1.8 copy-start.4
  88.5 249.6 %all-gather.3.cloned.1.call-start = ((), (), s32[]{:S(2)}) async-start(), calls=%async_computation.5 | async-start | bytes 8650752 | tf_op jit(solution)/shard_map/all_gather | solution.py:16
  122.2 4.1 copy-start.9
  122.2 227.6 %all-to-all-start.1 = ((bf16[32,2,12288]{2,1,0:T(2,128)(2,1)}), bf16[32,2,12288]{2,1,0:T(2,128)(2,1)S(1)}, u32[]{:S(2)}, u32[]{:S(2)}) async-start(bf16[32,2,12288]{2,1,0:T(2,128)(2,1)} %reshape.27), calls=%async_computation.2 | async-start | bytes 3145728 | tf_op jit(solution)/shard_map/all_to_all | solution.py:38
  338.1 6.0 %copy-start.10 = (bf16[512,8192]{1,0:T(8,128)(2,1)S(1)}, bf16[512,8192]{1,0:T(8,128)(2,1)}, u32[]{:S(2)}) copy-start(bf16[512,8192]{1,0:T(8,128)(2,1)} %all-gather.3.cloned.1.call-done) | copy-start | bytes 25165828
  349.8 1.1 copy-start.1
  351.0 32.8 %all-to-all-start.3 = ((bf16[8,512,256]{2,1,0:T(8,128)(2,1)}), bf16[8,512,256]{2,1,0:T(8,128)(2,1)S(1)}, u32[]{:S(2)}, u32[]{:S(2)}) async-start(bf16[8,512,256]{2,1,0:T(8,128)(2,1)} %bitcast.41), calls=%async_computation.4 | async-start | bytes 4194304 | tf_op jit(solution)/shard_map/all_to_all | solution.py:31
  355.8 155.0 %reduce-scatter.2.cloned.1.call-start = ((), (), s32[]{:S(2)}) async-start(), calls=%async_computation.7 | async-start | bytes 4325376 | tf_op jit(solution)/shard_map/reduce_scatter | solution.py:103
  383.7 64.0 %all-to-all-start.2 = ((bf16[8,512,512]{2,1,0:T(8,128)(2,1)}), bf16[8,512,512]{2,1,0:T(8,128)(2,1)}, u32[]{:S(2)}, u32[]{:S(2)}) async-start(bf16[8,512,512]{2,1,0:T(8,128)(2,1)} %bitcast.37), calls=%async_computation.3 | async-start | bytes 8388608 | tf_op jit(solution)/shard_map/all_to_all | solution.py:31
  450.7 2.9 copy-start
  450.7 2.9 copy-start.2
Sparse Core Ops, SparseCore 0:
  88.6 143.4 all-gather.4
  235.4 102.5 all-gather.2
  361.4 149.3 reduce-scatter.1
where the time goes:
time: 520 us; the launch traced here: 517 us
  waiting for transfers between devices  292 us (56%)
  local copies, waits for them, and re-layouts  123 us (24%)
  blocking collectives  36.1 us (7%)
  matrix products  23.1 us (4%)
  starting transfers between devices  17.4 us (3%)
  between operations  13.9 us (3%)
  other arithmetic  11.5 us (2%)
    all_gather x1, waiting for transfers between devices, local(): lax.all_gather(master.astype(jnp.bfloat16), 'fsdp', axis=0, tiled=True)  106 us
    all_gather x1, waiting for transfers between devices, sent_together(): lax.all_gather(both, axis, axis=dim, tiled=True)  95.1 us
    unnamed x26, local copies, waits for them, and re-layouts  62.3 us
    reduce_scatter x1, waiting for transfers between devices, local(): lax.psum_scatter(contract_last(hidden, down_weights).astype(jnp.bfloat16)...  53.1 us
    all_to_all x2, waiting for transfers between devices, sent_and_summed(): lax.all_to_all(parts, axis, split_axis=0, concat_axis=0, tiled=True)  38 us
    all_to_all x1, blocking collectives, local(): lax.all_to_all(master_all.astype(jnp.bfloat16), 'dp', split_axis=2, conca...  36.1 us
    all_to_all x1, local copies, waits for them, and re-layouts, in_one_piece(): lax.all_to_all(both, axis, split_axis=split_dim, concat_axis=concat_dim,...  15.1 us
    all_to_all x2, starting transfers between devices, sent_and_summed(): lax.all_to_all(parts, axis, split_axis=0, concat_axis=0, tiled=True)  13.2 us
  transfers between devices with their start and end apart: 6, of which 5 were waited for; matrix products, arithmetic and copies ran while one was open for 21% of the time, Pallas kernels for 0%

commit v1 on v0

--- a/solution.py
+++ b/solution.py
@@ -87,7 +87,11 @@
     master = lax.all_to_all(
         master_all.astype(jnp.bfloat16), "dp", split_axis=2, concat_axis=0, tiled=True
     ).astype(master_all.dtype)
-    weights = lax.all_gather(master.astype(jnp.bfloat16), "fsdp", axis=0, tiled=True)
+    x = master.astype(jnp.bfloat16)
+    n_dev = lax.axis_size("fsdp")
+    blocks = jnp.stack([x for _ in range(n_dev)])
+    blocks = lax.all_to_all(blocks, "fsdp", split_axis=0, concat_axis=0)
+    weights = jnp.concatenate(blocks, axis=0)
     rows_in, rows_back = sent_together((tokens, upstream), "dp", 0, 1)
     all_scales = jnp.concatenate([jnp.ones((old_master.shape[2],), jnp.float32), grow_mask])
     scales = lax.dynamic_slice_in_dim(all_scales, lax.axis_index("dp") * block_width, block_width)

time: 520 us -> 401 us (0.77)
  waiting for transfers between devices: 292 us -> 156 us
  starting transfers between devices: 17.4 us -> 27.3 us
    all_gather x1 -> x0, waiting for transfers between devices: 106 us -> none  [local(): lax.all_gather(master.astype(jnp.bfloat16), 'fsdp', axis=0, tiled=True)]
    all_gather x1, waiting for transfers between devices: 95.1 us -> 0.01 us  [sent_together(): lax.all_gather(both, axis, axis=dim, tiled=True)]
    all_to_all x0 -> x1, waiting for transfers between devices: none -> 50 us  [local(): blocks = lax.all_to_all(blocks, 'fsdp', split_axis=0, concat_axis=0)]
    all_to_all x1, waiting for transfers between devices: 0.01 us -> 19.4 us  [in_one_piece(): lax.all_to_all(both, axis, split_axis=split_dim, concat_axis=concat_dim,...]
    slice x2 -> x1, local copies, waits for them, and re-layouts: 10.9 us -> 2.32 us  [local(): paired = weights[:, :2, :].reshape(model_width, 2 * block_width)]
    all_to_all x0 -> x1, starting transfers between devices: none -> 5.42 us  [local(): blocks = lax.all_to_all(blocks, 'fsdp', split_axis=0, concat_axis=0)]
  transfers between devices with their start and end apart: 6 -> 6, of which waited for: 5 -> 5; matrix products, arithmetic and copies ran while one was open for 21% -> 39% of each run, Pallas kernels for 0% -> 0%
where the time goes in v1:
time: 401 us; the launch traced here: 399 us
  waiting for transfers between devices  156 us (39%)
  local copies, waits for them, and re-layouts  128 us (32%)
  blocking collectives  37.7 us (9%)
  starting transfers between devices  27.3 us (7%)
  matrix products  23.7 us (6%)
  between operations  14.2 us (4%)
  other arithmetic  11.6 us (3%)
    unnamed x26, local copies, waits for them, and re-layouts  66.5 us
    all_to_all x1, waiting for transfers between devices, local(): blocks = lax.all_to_all(blocks, 'fsdp', split_axis=0, concat_axis=0)  50 us
    reduce_scatter x1, waiting for transfers between devices, local(): lax.psum_scatter(contract_last(hidden, down_weights).astype(jnp.bfloat16)...  49.8 us
    all_to_all x1, blocking collectives, local(): lax.all_to_all(master_all.astype(jnp.bfloat16), 'dp', split_axis=2, conca...  37.7 us
    all_to_all x2, waiting for transfers between devices, sent_and_summed(): lax.all_to_all(parts, axis, split_axis=0, concat_axis=0, tiled=True)  36.7 us
    all_to_all x1, waiting for transfers between devices, in_one_piece(): lax.all_to_all(both, axis, split_axis=split_dim, concat_axis=concat_dim,...  19.4 us
    all_to_all x2, starting transfers between devices, sent_and_summed(): lax.all_to_all(parts, axis, split_axis=0, concat_axis=0, tiled=True)  15.9 us
    all_to_all x1, local copies, waits for them, and re-layouts, in_one_piece(): lax.all_to_all(both, axis, split_axis=split_dim, concat_axis=concat_dim,...  15.2 us
  transfers between devices with their start and end apart: 6, of which 5 were waited for; matrix products, arithmetic and copies ran while one was open for 39% of the time, Pallas kernels for 0%

profile of v1, /device:TPU:4, one launch (start us, length us, event | category | flops | bytes accessed | tf_op | source)
XLA Modules:
  0.0 398.5 jit_solution(1494171777432167430)
XLA Ops:
  7.2 0.0 copy-start.3
  7.2 0.0 all-gather.2.cloned.1.call-start
  7.2 1.8 pad_maximum_fusion.2
  9.0 0.0 all-gather.2.cloned.1.call-update
  9.0 1.1 convert.19
  10.1 0.0 copy-done.3
  10.1 0.1 convert.18
  10.1 0.1 pad_maximum_fusion.1
  10.2 8.3 %copy.45 = bf16[16,3,8192]{0,1,2:T(4,128)(2,1)} copy(bf16[16,3,8192]{2,0,1:T(8,128)(2,1)S(1)} %pad_maximum_fusion.1) | data formatting | bytes 1572864 | tf_op jit(solution)/shard_map/concatenate | solution.py:84
  18.5 12.8 %reshape.32 = bf16[32,2,6144]{2,1,0:T(2,128)(2,1)S(1)} reshape(bf16[8192,3,16]{2,1,0:T(4,128)(2,1)} %bitcast.37) | data formatting | bytes 1572864
  31.3 37.7 %all_to_all.48 = bf16[32,2,6144]{2,1,0:T(2,128)(2,1)S(1)} all-to-all(bf16[32,2,6144]{2,1,0:T(2,128)(2,1)S(1)} %reshape.32), channel_id=1, replica_groups=mesh['dp'=32,'fsdp'=8] {'dp'}, dimensions={0} | all-to-all | bytes 1572864 | tf_op jit(solution)/shard_map/all_to_all | solution.py:87
  69.0 10.8 %reshape.33 = bf16[8192,3,16]{2,1,0:T(4,128)(2,1)} reshape(bf16[32,2,6144]{2,1,0:T(2,128)(2,1)S(1)} %all_to_all.48) | data formatting | bytes 1572864
  79.8 10.0 %copy.57 = bf16[16,3,32,256]{3,0,2,1:T(8,128)(2,1)S(1)} copy(bf16[16,3,32,256]{0,1,3,2:T(4,128)(2,1)} %bitcast.38) | data formatting | bytes 1572864 | tf_op jit(solution)/shard_map/all_to_all | solution.py:87
  89.9 0.3 copy.48
  90.2 3.4 stack.5
  93.6 0.0 copy-start.6
  93.6 0.0 copy-start.4
  93.6 5.4 %all-to-all-start.1 = ((bf16[8,512,3,256]{1,3,2,0:T(8,128)(2,1)}), bf16[8,512,3,256]{1,3,2,0:T(8,128)(2,1)}, u32[]{:S(2)}, u32[]{:S(2)}) async-start(bf16[8,512,3,256]{1,3,2,0:T(8,128)(2,1)} %stack.5), calls=%async_computation.1 | async-start | bytes 12582912 | tf_op jit(solution)/shard_map/all_to_all | solution.py:93
  99.0 0.0 copy-done.6
  99.0 0.0 copy-start.5
  99.0 0.0 copy-done.4
  99.1 0.1 convert.22
  99.1 0.9 copy-done.7
  100.1 0.3 copy-done.5
  100.4 0.1 convert.20
  100.4 0.1 maximum_maximum_fusion
  100.6 13.1 %copy.51 = bf16[16,6,8192]{0,1,2:T(8,128)(2,1)} copy(bf16[16,6,8192]{2,0,1:T(8,128)(2,1)S(1)} %maximum_maximum_fusion) | data formatting | bytes 3145728 | tf_op jit(solution)/shard_map/concatenate | solution.py:36
  113.7 18.9 %reshape.34 = bf16[32,2,12288]{2,1,0:T(2,128)(2,1)} reshape(bf16[8192,6,16]{2,1,0:T(8,128)(2,1)} %bitcast.35) | data formatting | bytes 3145728
  132.5 0.0 copy-start.8
  132.5 50.0 %all-to-all-done.1 = bf16[8,512,3,256]{1,3,2,0:T(8,128)(2,1)} async-done(((bf16[8,512,3,256]{1,3,2,0:T(8,128)(2,1)}), bf16[8,512,3,256]{1,3,2,0:T(8,128)(2,1)}, u32[]{:S(2)}, u32[]{:S(2)}) %all-to-all-start.1) | async-done | bytes 6291488 | tf_op jit(solution)/shard_map/all_to_all | solution.py:93
  182.5 6.0 %all-to-all-start.2 = ((bf16[32,2,12288]{2,1,0:T(2,128)(2,1)}), bf16[32,2,12288]{2,1,0:T(2,128)(2,1)S(1)}, u32[]{:S(2)}, u32[]{:S(2)}) async-start(bf16[32,2,12288]{2,1,0:T(2,128)(2,1)} %reshape.34), calls=%async_computation.3 | async-start | bytes 3145728 | tf_op jit(solution)/shard_map/all_to_all | solution.py:38
  188.5 0.0 copy-done.8
  188.5 0.1 pad_dynamic-slice_fusion
  188.6 3.7 copy.60
  192.3 0.0 copy-start
  192.3 2.7 copy-done
  195.0 2.3 slice.33
  197.3 0.0 all-gather.2.cloned.1.call-done
  197.3 0.0 copy-start.9
  197.3 6.0 %fusion.4 = f32[512,512]{0,1:T(8,128)S(1)} fusion(bf16[4096,512]{0,1:T(8,128)(2,1)} %bitcast.45, bf16[512,8192]{1,0:T(8,128)(2,1)} %all-gather.2.cloned.1.call-done), kind=kOutput, calls=%fused_computation.9 | convolution fusion | flops 2147483648 | bytes 9437184 | tf_op jit(solution)/shard_map/dot_general | solution.py:101
  203.3 0.0 copy-done.9
  203.3 3.7 multiply_convert_fusion.1
  207.0 2.7 convolution_convert_fusion.2
  209.7 19.4 %all-to-all-done.2 = bf16[32,2,12288]{2,1,0:T(2,128)(2,1)S(1)} async-done(((bf16[32,2,12288]{2,1,0:T(2,128)(2,1)}), bf16[32,2,12288]{2,1,0:T(2,128)(2,1)S(1)}, u32[]{:S(2)}, u32[]{:S(2)}) %all-to-all-start.2) | async-done | bytes 1572896 | tf_op jit(solution)/shard_map/all_to_all | solution.py:38
  229.1 0.0 copy-start.1
  229.1 1.1 copy-done.1
  230.2 7.5 %all-to-all-start.4 = ((bf16[8,512,256]{2,1,0:T(8,128)(2,1)}), bf16[8,512,256]{2,1,0:T(8,128)(2,1)S(1)}, u32[]{:S(2)}, u32[]{:S(2)}) async-start(bf16[8,512,256]{2,1,0:T(8,128)(2,1)} %bitcast.48), calls=%async_computation.5 | async-start | bytes 4194304 | tf_op jit(solution)/shard_map/all_to_all | solution.py:31
  237.7 0.0 reduce-scatter.2.cloned.1.call-start
  237.7 4.8 %convolution_convert_fusion = bf16[512,4096]{1,0:T(8,128)(2,1)} fusion(bf16[512,256]{0,1:T(8,128)(2,1)S(1)} %get-tuple-element.13, bf16[4096,3,256]{0,2,1:T(8,128)(2,1)} %bitcast.41), kind=kOutput, calls=%fused_computation.1 | convolution fusion | flops 1075838976 | bytes 6553600 | tf_op jit(solution)/shard_map/dot_general | solution.py:55
  242.6 0.0 reduce-scatter.2.cloned.1.call-update
  242.6 0.9 copy-done.10
  243.5 6.5 %convolution_convert_fusion.1 = bf16[4096,512]{1,0:T(8,128)(2,1)} fusion(bf16[512,8192]{1,0:T(8,128)(2,1)} %all-gather.2.cloned.1.call-done, bf16[512,256]{0,1:T(8,128)(2,1)S(1)} %copy-done.10, bf16[512,256]{0,1:T(8,128)(2,1)S(1)} %get-tuple-element.11), kind=kOutput, calls=%fused_computation.2 | convolution fusion | flops 2150629376 | bytes 8912896 | tf_op jit(solution)/shard_map/dot_general | solution.py:49
  250.1 14.7 %all-to-all-done.4 = bf16[8,512,256]{2,1,0:T(8,128)(2,1)S(1)} async-done(((bf16[8,512,256]{2,1,0:T(8,128)(2,1)}), bf16[8,512,256]{2,1,0:T(8,128)(2,1)S(1)}, u32[]{:S(2)}, u32[]{:S(2)}) %all-to-all-start.4) | async-done | bytes 2097184 | tf_op jit(solution)/shard_map/all_to_all | solution.py:31
  264.8 8.4 %all-to-all-start.3 = ((bf16[8,512,512]{2,1,0:T(8,128)(2,1)}), bf16[8,512,512]{2,1,0:T(8,128)(2,1)}, u32[]{:S(2)}, u32[]{:S(2)}) async-start(bf16[8,512,512]{2,1,0:T(8,128)(2,1)} %bitcast.44), calls=%async_computation.4 | async-start | bytes 8388608 | tf_op jit(solution)/shard_map/all_to_all | solution.py:31
  273.1 18.0 %reshape.35 = bf16[8192,6,16]{2,1,0:T(8,128)(2,1)} reshape(bf16[32,2,12288]{2,1,0:T(2,128)(2,1)} %copy-done.1) | data formatting | bytes 3145728
  291.1 15.2 %copy.53 = bf16[32,16,6,256]{3,1,0,2:T(8,128)(2,1)} copy(bf16[32,16,6,256]{1,2,3,0:T(8,128)(2,1)} %bitcast.36) | data formatting | bytes 3145728 | tf_op jit(solution)/shard_map/all_to_all | solution.py:38
  306.3 0.3 convert_reduce_fusion.1
  306.6 21.9 %all-to-all-done.3 = bf16[8,512,512]{2,1,0:T(8,128)(2,1)} async-done(((bf16[8,512,512]{2,1,0:T(8,128)(2,1)}), bf16[8,512,512]{2,1,0:T(8,128)(2,1)}, u32[]{:S(2)}, u32[]{:S(2)}) %all-to-all-start.3) | async-done | bytes 4194336 | tf_op jit(solution)/shard_map/all_to_all | solution.py:31
  328.6 3.8 convert_reduce_fusion
  332.4 2.7 copy.54
  335.1 2.5 copy.55
  337.6 0.0 copy-done.2
  337.6 4.2 %convert_subtract_fusion = (f32[512,3,256]{2,0,1:T(8,128)}, f32[512,3,256]{2,0,1:T(8,128)}, f32[512,3,256]{2,0,1:T(8,128)}) fusion(bf16[16,3,32,256]{3,0,2,1:T(8,128)(2,1)S(1)} %copy.57, f32[512,1,256]{2,0,1:T(8,128)S(1)} %bitcast.47, f32[512,2,256]{2,0,1:T(8,128)} %copy.55, bf16[512,6,256]{2,0,1:T(8,128)(2,1)S(1)} %bitcast.43), kind=kLoop, calls=%fused_computation.13 | loop fusion | flops 7077888 | bytes 8650752 | tf_op jit(solution)/shard_map/sub | solution.py:65
  341.9 49.8 %reduce-scatter.2.cloned.1.call-done = bf16[16,4096]{1,0:T(8,128)(2,1)} async-done(((bf16[512,4096]{1,0:T(8,128)(2,1)}), bf16[16,4096]{1,0:T(8,128)(2,1)}) %reduce-scatter.2.cloned.1.call-update) | async-done | bytes 131088 | tf_op jit(solution)/shard_map/reduce_scatter | solution.py:107
  (5 shorter events, 0.1 us)
Async XLA Ops:
  7.2 2.9 copy-start.3
  7.2 190.1 %all-gather.2.cloned.1.call-start = ((), (), s32[]{:S(2)}) async-start(), calls=%async_computation.6 | async-start | bytes 8650752 | tf_op jit(solution)/shard_map/all_gather | solution.py:16
  93.6 5.4 %copy-start.6 = (f32[16,3,2560]{2,0,1:T(8,128)S(1)}, f32[16,3,2560]{2,0,1:T(8,128)}, u32[]{:S(2)}) copy-start(f32[16,3,2560]{2,0,1:T(8,128)} %param.16) | copy-start | bytes 1474564
  93.6 5.5 %copy-start.4 = (f32[16,3,5632]{2,0,1:T(8,128)S(1)}, f32[16,3,5632]{2,0,1:T(8,128)}, u32[]{:S(2)}) copy-start(f32[16,3,5632]{2,0,1:T(8,128)} %param.13) | copy-start | bytes 3244036
  93.6 88.9 %all-to-all-start.1 = ((bf16[8,512,3,256]{1,3,2,0:T(8,128)(2,1)}), bf16[8,512,3,256]{1,3,2,0:T(8,128)(2,1)}, u32[]{:S(2)}, u32[]{:S(2)}) async-start(bf16[8,512,3,256]{1,3,2,0:T(8,128)(2,1)} %stack.5), calls=%async_computation.1 | async-start | bytes 12582912 | tf_op jit(solution)/shard_map/all_to_all | solution.py:93
  99.0 1.0 copy-start.7
  99.0 1.4 copy-start.5
  132.5 55.9 %copy-start.8 = (f32[2560]{0:T(1024)S(1)}, f32[2560]{0:T(1024)}, u32[]{:S(2)}) copy-start(f32[2560]{0:T(1024)} %param.17) | copy-start | bytes 30724
  182.5 46.6 %all-to-all-start.2 = ((bf16[32,2,12288]{2,1,0:T(2,128)(2,1)}), bf16[32,2,12288]{2,1,0:T(2,128)(2,1)S(1)}, u32[]{:S(2)}, u32[]{:S(2)}) async-start(bf16[32,2,12288]{2,1,0:T(2,128)(2,1)} %reshape.34), calls=%async_computation.3 | async-start | bytes 3145728 | tf_op jit(solution)/shard_map/all_to_all | solution.py:38
  192.3 2.7 copy-start
  197.3 6.0 %copy-start.9 = (bf16[512,8192]{1,0:T(8,128)(2,1)S(1)}, bf16[512,8192]{1,0:T(8,128)(2,1)}, u32[]{:S(2)}) copy-start(bf16[512,8192]{1,0:T(8,128)(2,1)} %all-gather.2.cloned.1.call-done) | copy-start | bytes 25165828
  229.1 1.1 copy-start.1
  230.2 34.5 %all-to-all-start.4 = ((bf16[8,512,256]{2,1,0:T(8,128)(2,1)}), bf16[8,512,256]{2,1,0:T(8,128)(2,1)S(1)}, u32[]{:S(2)}, u32[]{:S(2)}) async-start(bf16[8,512,256]{2,1,0:T(8,128)(2,1)} %bitcast.48), calls=%async_computation.5 | async-start | bytes 4194304 | tf_op jit(solution)/shard_map/all_to_all | solution.py:31
  237.7 154.0 %reduce-scatter.2.cloned.1.call-start = ((), (), s32[]{:S(2)}) async-start(), calls=%async_computation.7 | async-start | bytes 4325376 | tf_op jit(solution)/shard_map/reduce_scatter | solution.py:107
  242.6 0.9 copy-start.10
  264.8 63.8 %all-to-all-start.3 = ((bf16[8,512,512]{2,1,0:T(8,128)(2,1)}), bf16[8,512,512]{2,1,0:T(8,128)(2,1)}, u32[]{:S(2)}, u32[]{:S(2)}) async-start(bf16[8,512,512]{2,1,0:T(8,128)(2,1)} %bitcast.44), calls=%async_computation.4 | async-start | bytes 8388608 | tf_op jit(solution)/shard_map/all_to_all | solution.py:31
  332.4 5.2 %copy-start.2 = (bf16[32,16,6,256]{3,1,0,2:T(8,128)(2,1)S(1)}, bf16[32,16,6,256]{3,1,0,2:T(8,128)(2,1)}, u32[]{:S(2)}) copy-start(bf16[32,16,6,256]{3,1,0,2:T(8,128)(2,1)} %copy.53) | copy-start | bytes 4718596
Sparse Core Ops, SparseCore 0:
  11.3 108.8 all-gather.1
  243.3 148.3 reduce-scatter.1
